TPU v7x, 32 devices: a whole 2x2x4 slice. The times are simulated.
32 devices in a mesh: dom: 16 (over z, y, core), vol: 2 (over x).
Axes of the slice: x: 2, y: 2, z: 4, core: 2. Of those that a mesh axis runs over, the one named last changes fastest.
Arguments:
- images: bfloat16 [8192, 2, 2048], P('dom', None, 'vol'), may hold values from -8 to 8
- ctf_gain: bfloat16 [8192, 2048], P('dom', 'vol'), may hold values from -1 to 1
- orientation: int32 [8192, 8], P('dom'), may hold values from 0 to 15
- class_ids: int32 [8192, 8], P('dom'), may hold values from 0 to 15
- slice_index: int32 [16, 2048], P(None, 'vol'), may hold values from 0 to 131071, as said below
- volume: bfloat16 [16, 2, 2, 65536], P(None, None, 'vol', 'dom'), may hold values from -5 to 5
- noise_power: float32 [2048], P('vol'), may hold values from 40 to 160
- log_prior: float32 [16], replicated, may hold values from -1.5 to 1.5
- prior_precision: float32 [2, 65536], P('vol', 'dom'), may hold values from 0.5 to 4
Outputs:
- new_volume: bfloat16 [16, 2, 2, 65536], P(None, None, 'vol', 'dom')
- noise_update: float32 [2048], P('vol')
- occupancy: float32 [16], replicated
Inputs may be any that keep to these rules, and one draw needn't show every extreme that they name: `slice_index`: the coefficients of band b, columns b * 1024 to (b + 1) * 1024 - 1, map to voxels b * 65536 to (b + 1) * 65536 - 1.
All inputs are finite; a program needn't handle non-finite values.
Results may differ from a plain program's by a relative error of at most 0.012.
Values may be sent and summed in bfloat16 or wider, within the bound.
A program may use at most 128 MiB of HBM per device.

v0:
```python
import jax
import jax.numpy as jnp
from jax import lax
from jax.sharding import PartitionSpec as P


def shards(
    images,
    ctf_gain,
    orientation,
    class_ids,
    slice_index,
    volume,
    noise_power,
    log_prior,
    prior_precision,
):
    groups = lax.axis_size("dom")
    part_dev = images.shape[0]
    shell_pix = images.shape[2]
    classes = volume.shape[0]
    vox_dev = volume.shape[3]
    orient_count = slice_index.shape[0]
    hypo_count = classes * orient_count
    shell_vox = vox_dev * groups
    band_start = lax.axis_index("vol") * shell_vox
    local_index = slice_index - band_start
    image_f32 = images.astype(jnp.float32)
    gain_f32 = ctf_gain.astype(jnp.float32)
    weighted = (
        (gain_f32[:, None, :] * image_f32 / noise_power)
        .astype(jnp.bfloat16)
        .reshape(part_dev, 2 * shell_pix)
    )
    damped = (gain_f32 * gain_f32 / (2.0 * noise_power)).astype(jnp.bfloat16)
    carried = (
        (gain_f32[:, None, :] * image_f32).astype(jnp.bfloat16).reshape(part_dev, 2 * shell_pix)
    )
    gain_square = (gain_f32 * gain_f32).astype(jnp.bfloat16)
    gathered = lax.all_gather(volume[:, :, 0, :], "dom", axis=2, tiled=True)
    slices = jnp.take(gathered, local_index, axis=2)
    projected = jnp.transpose(slices, (0, 2, 1, 3)).reshape(hypo_count, 2 * shell_pix)
    power_table = (
        jnp.sum(jnp.square(slices.astype(jnp.float32)), axis=1)
        .reshape(hypo_count, shell_pix)
        .astype(jnp.bfloat16)
    )
    contract_last = (((1,), (1,)), ((), ()))
    cross_term = lax.dot_general(
        weighted, projected, contract_last, preferred_element_type=jnp.float32
    )
    energy = lax.dot_general(damped, power_table, contract_last, preferred_element_type=jnp.float32)
    hypothesis = class_ids * orient_count + orientation
    partial_value = jnp.take_along_axis(cross_term - energy, hypothesis, axis=1)
    fitted = lax.psum(partial_value, "vol")
    scores = log_prior[class_ids] + fitted
    posterior = jax.nn.softmax(scores, axis=1)
    hypo_ids = jnp.arange(hypo_count, dtype=jnp.int32)
    matches = (hypothesis[:, :, None] == hypo_ids[None, None, :]).astype(jnp.float32)
    member_blocks = jnp.sum(posterior[:, :, None] * matches, axis=1)
    member_bf16 = member_blocks.astype(jnp.bfloat16)
    contract_first = (((0,), (0,)), ((), ()))
    sums_data = lax.dot_general(
        member_bf16, carried, contract_first, preferred_element_type=jnp.float32
    )
    sums_weight = lax.dot_general(
        member_bf16, gain_square, contract_first, preferred_element_type=jnp.float32
    )
    mean_proj = jnp.dot(member_bf16, projected, preferred_element_type=jnp.float32).reshape(
        part_dev, 2, shell_pix
    )
    mean_power = jnp.dot(member_bf16, power_table, preferred_element_type=jnp.float32)
    residual = (
        jnp.sum(image_f32 * image_f32, axis=1)
        - 2.0 * gain_f32 * jnp.sum(image_f32 * mean_proj, axis=1)
        + gain_f32 * gain_f32 * mean_power
    )
    noise_part = jnp.sum(residual, axis=0)
    occupancy_part = jnp.sum(member_blocks.reshape(part_dev, classes, orient_count), axis=(0, 2))
    noise_sum, occupancy_sum = lax.psum((noise_part, occupancy_part), "dom")
    particles = part_dev * groups
    noise_update = noise_sum / (2.0 * particles)
    occupancy = occupancy_sum / particles
    data_rows = jnp.transpose(
        sums_data.reshape(classes, orient_count, 2, shell_pix), (0, 2, 1, 3)
    ).reshape(2 * classes, orient_count * shell_pix)
    weight_rows = sums_weight.reshape(classes, orient_count * shell_pix)
    values = jnp.concatenate([data_rows, weight_rows], axis=0)
    flat_index = local_index.reshape(-1)
    voxel_rows = jax.ops.segment_sum(values.T, flat_index, num_segments=shell_vox)
    owned = lax.psum_scatter(voxel_rows.T, "dom", scatter_dimension=1, tiled=True)
    data_sum = owned[: 2 * classes].reshape(classes, 2, vox_dev)
    weight_sum = owned[2 * classes :]
    denominator = weight_sum + prior_precision[0][None, :]
    new_volume = (data_sum / denominator[:, None, :]).astype(jnp.bfloat16)[:, :, None, :]
    return (new_volume, noise_update, occupancy)


def solution(mesh):
    in_specs = (
        P("dom", None, "vol"),
        P("dom", "vol"),
        P("dom", None),
        P("dom", None),
        P(None, "vol"),
        P(None, None, "vol", "dom"),
        P("vol"),
        P(),
        P("vol", "dom"),
    )
    out_specs = (P(None, None, "vol", "dom"), P("vol"), P())
    return jax.shard_map(shards, mesh=mesh, in_specs=in_specs, out_specs=out_specs, check_vma=False)
```

profile of v0, /device:TPU:0, one launch (start us, length us, event | category | flops | bytes accessed | tf_op | source)
XLA Modules:
  0.0 730.4 jit_solution(9205712266040504341)
XLA Ops:
  7.2 1.8 copy.83
  9.1 1.0 fusion.12
  10.1 1.5 convert_element_type.45
  11.6 4.0 fusion.2
  15.6 4.0 copy.82
  20.0 2.6 copy.90
  23.5 40.6 %all-gather.3.cloned.1.call-done = bf16[16,2,1,65536]{3,0,2,1:T(8,128)(2,1)} async-done(((bf16[16,2,1,4096]{3,0,2,1:T(8,128)(2,1)}), bf16[16,2,1,65536]{3,0,2,1:T(8,128)(2,1)}) %all-gather.3.cloned.1.call-update) | async-done | bytes 4194320 | tf_op jit(solution)/shard_map/all_gather | solution.py:40
  64.1 60.3 %copy.84 = bf16[16,2,1,65536]{0,1,3,2:T(2,128)(2,1)} copy(bf16[16,2,1,65536]{3,0,2,1:T(8,128)(2,1)} %all-gather.3.cloned.1.call-done) | data formatting | bytes 8388608 | tf_op jit(solution)/shard_map/all_gather | solution.py:40
  124.4 246.3 %gather_fusion = bf16[16384,16,2]{1,2,0:T(2,128)(2,1)} fusion(bf16[16,2,65536]{0,1,2:T(2,128)(2,1)} %bitcast.76, s32[16384]{0:T(1024)S(1)} %broadcast_clamp_fusion), kind=kCustom, calls=%fused_computation | custom fusion | bytes 2162688 | tf_op jit(solution)/shard_map/jit(_take)/gather | solution.py:41
  370.6 19.0 %copy.85 = bf16[16,1024,16,2]{1,3,0,2:T(2,128)(2,1)S(1)} copy(bf16[16,1024,16,2]{2,3,1,0:T(2,128)(2,1)} %bitcast.77) | data formatting | bytes 2097152 | tf_op jit(solution)/shard_map/jit(_take)/gather | solution.py:41
  389.6 3.6 multiply_reduce_fusion
  393.6 0.8 fusion.17
  395.6 32.8 %gather_fusion.1 = f32[4096]{0:T(1024)S(1)} fusion(f32[512,256]{1,0:T(8,128)S(1)} %convolution_subtract_fusion, s32[4096]{0:T(1024)S(1)} %reshape.106), kind=kCustom, calls=%fused_computation.1 | custom fusion | bytes 65536 | tf_op jit(solution)/shard_map/jit(take_along_axis)/gather | solution.py:54
  428.7 8.1 %psum.21 = f32[512,8]{0,1:T(8,128)S(1)} all-reduce(f32[512,8]{0,1:T(8,128)S(1)} %and_select_fusion), channel_id=1, replica_groups=mesh['dom'=16,'vol'=2] {'vol'}, use_global_device_ids=true, to_apply=%region_1.2 | all-reduce | flops 4096 | bytes 32768 | tf_op jit(solution)/shard_map/psum | solution.py:55
  436.8 10.1 %fusion.15 = (f32[512]{0:T(512)S(1)}, f32[512,8]{0,1:T(8,128)S(1)}) fusion(f32[512,8]{0,1:T(8,128)S(1)} %psum.21, f32[]{:T(128)} %bitcast.15, f32[]{:T(128)} %bitcast.14, f32[]{:T(128)} %bitcast.13, f32[]{:T(128)} %bitcast.12, f32[]{:T(128)} %bitcast.11, f32[]{:T(128)} %bitcast.10, f32[]{:T(128)} %bitcast.9, f32[]{:T(128)} %bitcast.8, f32[]{:T(128)} %bitcast.7, ...), kind=kLoop, calls=%fused_computation.47 | loop fusion | flops 142848 | bytes 51264 | tf_op jit(solution)/shard_map/reduce_max | solution.py:57
  447.0 3.2 select_reduce_fusion
  450.9 2.3 fusion.7
  453.2 2.6 copy.100
  455.8 1.2 reshape.73
  457.0 2.1 maximum_bitcast_fusion
  459.1 4.7 copy.91
  463.8 100.8 %scatter_custom_fusion = f32[65536,48]{1,0:T(8,128)} fusion(s32[16384]{0:T(1024)S(1)} %bitcast.90, f32[16384,48]{1,0:T(8,128)} %copy.91, f32[]{:T(128)} %constant.16.clone.1), kind=kCustom, calls=%fused_computation.3 | custom fusion | flops 786432 | bytes 12583424 | tf_op jit(solution)/shard_map/scatter-add | solution.py:90
  564.6 23.1 %copy.92 = f32[65536,48]{0,1:T(8,128)} copy(f32[65536,48]{1,0:T(8,128)} %scatter_custom_fusion) | data formatting | bytes 25165824 | tf_op jit(solution)/shard_map/scatter-add | solution.py:90
  587.7 1.2 copy-done.4
  588.9 1.3 copy.96
  590.4 3.0 fusion.6
  593.4 0.7 add_reduce_fusion
  594.2 30.2 %all-reduce = (f32[1024]{0:T(1024)S(1)}, f32[16]{0:T(128)S(1)}) all-reduce(f32[1024]{0:T(1024)S(1)} %add_reduce_fusion, f32[16]{0:T(128)S(1)} %reduce_sum.78), channel_id=1, replica_groups=mesh['dom'=16,'vol'=2] {'dom'}, use_global_device_ids=true, to_apply=%region_10.11 | all-reduce | flops 1040 | bytes 8320 | tf_op jit(solution)/shard_map/psum | solution.py:80
  625.5 94.7 %reduce-scatter.2.cloned.1.call-done = f32[48,4096]{1,0:T(8,128)} async-done(((f32[48,65536]{1,0:T(8,128)}), f32[48,4096]{1,0:T(8,128)}) %reduce-scatter.2.cloned.1.call-update) | async-done | bytes 786448 | tf_op jit(solution)/shard_map/reduce_scatter | solution.py:91
  720.2 1.1 slice.29
  721.6 1.0 slice_add_fusion
  722.6 1.0 fusion.11
  (60 shorter events, 5.6 us)
Async XLA Ops:
  7.2 4.4 copy-start.13
  7.2 56.9 %all-gather.3.cloned.1.call-start = ((), (), s32[]{:S(2)}) async-start(), calls=%async_computation.2 | async-start | bytes 4456448 | tf_op jit(solution)/shard_map/all_gather | solution.py:40
  9.0 711.2 %reduce-scatter.2.cloned.1.call-start = ((), (), s32[]{:S(2)}) async-start(), calls=%async_computation.1 | async-start | bytes 13369344 | tf_op jit(solution)/shard_map/reduce_scatter | solution.py:91
  9.1 2.5 copy-start.5
  15.6 4.0 copy-start.12
  15.6 4.0 copy-start.15
  20.0 2.7 copy-start.11
  20.0 3.4 copy-start.10
  389.6 3.9 copy-start.9
  393.2 1.1 copy-start.7
  393.5 1.0 copy-start.3
  393.5 1.6 copy-start
  587.7 1.2 copy-start.4
  587.7 2.7 copy-start.6
  590.4 3.0 copy-start.1
  590.4 3.0 copy-start.2
  590.4 3.0 copy-start.8
  594.2 127.4 %copy-start.14 = (f32[1,4096]{1,0:T(1,128)S(1)}, f32[1,4096]{1,0:T(1,128)}, u32[]{:S(2)}) copy-start(f32[1,4096]{1,0:T(1,128)} %param.17) | copy-start | bytes 49156
Sparse Core Ops, SparseCore 0:
  10.8 53.2 all-gather.2
  587.8 132.3 reduce-scatter.1
where the time goes:
time: 740 us; the launch traced here: 730 us
  local copies, waits for them, and re-layouts  405 us (55%)
  waiting for transfers between devices  135 us (18%)
  other arithmetic  130 us (18%)
  blocking collectives  38.3 us (5%)
  between operations  14.4 us (2%)
  matrix products  7.74 us (1%)
    gather x2, local copies, waits for them, and re-layouts, shards(): slices = jnp.take(gathered, local_index, axis=2)  265 us
    scatter-add x1, other arithmetic, shards(): jax.ops.segment_sum(values.T, flat_index, num_segments=shell_vox)  101 us
    reduce_scatter x1, waiting for transfers between devices, shards(): lax.psum_scatter(voxel_rows.T, 'dom', scatter_dimension=1, tiled=True)  94.7 us
    all_gather x1, local copies, waits for them, and re-layouts, shards(): gathered = lax.all_gather(volume[:, :, 0, :], 'dom', axis=2, tiled=True)  60.3 us
    all_gather x1, waiting for transfers between devices, shards(): gathered = lax.all_gather(volume[:, :, 0, :], 'dom', axis=2, tiled=True)  40.6 us
    gather x5, local copies, waits for them, and re-layouts, shards(): partial_value = jnp.take_along_axis(cross_term - energy, hypothesis, axis=1)  33.3 us
    psum x1, blocking collectives, shards(): noise_sum, occupancy_sum = lax.psum((noise_part, occupancy_part), 'dom')  30.2 us
    scatter-add x1, local copies, waits for them, and re-layouts, shards(): jax.ops.segment_sum(values.T, flat_index, num_segments=shell_vox)  23.1 us
  transfers between devices with their start and end apart: 2, of which 2 were waited for; matrix products, arithmetic and copies ran while one was open for 3% of the time, Pallas kernels for 0%

commit v1 on v0

v1 whole, which is shorter than its diff:
```python
import functools

import jax
import jax.numpy as jnp
from jax import lax
from jax.experimental import pallas as pl
from jax.experimental.pallas import tpu as pltpu
from jax.sharding import PartitionSpec as P

LANES = 256
BIG = 48 << 20
NT = (((1,), (1,)), ((), ()))


def voxel_base(shell_vox, vox_dev):
    return lax.axis_index("vol") * shell_vox + lax.axis_index("dom") * vox_dev


def gather_kernel(shell_vox, vox_dev, index_ref, vol_ref, out_ref, stack_ref):
    orient = pl.program_id(0)
    groups = vox_dev // LANES
    rows = vol_ref.shape[0]

    @pl.when(orient == 0)
    def _():
        for q in range(groups):
            stack_ref[q * rows : (q + 1) * rows, :] = vol_ref[:, q * LANES : (q + 1) * LANES]

    rel = index_ref[pl.ds(orient, 1), :] - voxel_base(shell_vox, vox_dev)
    low = rel & (LANES - 1)
    high = rel >> 8
    pix = rel.shape[1]
    step = 256
    for start in range(0, pix, step):
        low_c = low[:, start : start + step]
        high_c = high[:, start : start + step]
        hot = jnp.where(
            lax.broadcasted_iota(jnp.int32, (LANES, step), 0) == low_c, 1.0, 0.0
        ).astype(jnp.bfloat16)
        found = jnp.dot(stack_ref[...], hot, preferred_element_type=jnp.float32)
        total = jnp.zeros((rows, step), jnp.float32)
        for q in range(groups):
            total = jnp.where(high_c == q, found[q * rows : (q + 1) * rows], total)
        half = rows // 2
        out_ref[0, 0, :, start : start + step] = total[:half].astype(jnp.bfloat16)
        out_ref[1, 0, :, start : start + step] = total[half:].astype(jnp.bfloat16)


def fit_kernel(proj_ref, weighted_ref, damped_ref, hypo_ref, out_ref):
    p0 = proj_ref[0]
    p1 = proj_ref[1]
    f0 = p0.astype(jnp.float32)
    f1 = p1.astype(jnp.float32)
    power = (f0 * f0 + f1 * f1).astype(jnp.bfloat16)
    value = lax.dot_general(p0, weighted_ref[0], NT, preferred_element_type=jnp.float32)
    value += lax.dot_general(p1, weighted_ref[1], NT, preferred_element_type=jnp.float32)
    value -= lax.dot_general(power, damped_ref[...], NT, preferred_element_type=jnp.float32)
    ids = lax.broadcasted_iota(jnp.int32, value.shape, 0)
    for k in range(hypo_ref.shape[0]):
        out_ref[k : k + 1, :] = jnp.sum(
            jnp.where(hypo_ref[k : k + 1, :] == ids, value, 0.0), axis=0, keepdims=True
        )


def member_kernel(
    prior_ref, fit_ref, hypo_ref, proj_ref, carried_ref, square_ref, energy_ref,
    table_ref, noise_ref, occ_ref,
):
    hypo = hypo_ref[...]
    classes = prior_ref.shape[0]
    class_of = lax.rem(hypo, classes)
    scores = fit_ref[...]
    for c in range(classes):
        scores += jnp.where(class_of == c, prior_ref[c], 0.0)
    top = jnp.max(scores, axis=0, keepdims=True)
    expo = jnp.exp(scores - top)
    posterior = expo / jnp.sum(expo, axis=0, keepdims=True)
    count = proj_ref.shape[1]
    ids = lax.broadcasted_iota(jnp.int32, (count, hypo.shape[1]), 0)
    member = jnp.zeros(ids.shape, jnp.float32)
    for k in range(hypo.shape[0]):
        member += jnp.where(hypo[k : k + 1, :] == ids, posterior[k : k + 1, :], 0.0)
    occ = jnp.sum(member, axis=1, keepdims=True)
    occ_ref[...] = jnp.sum(occ.reshape(count // classes, classes, 1), axis=0)
    member16 = member.astype(jnp.bfloat16)
    pix = square_ref.shape[1]
    step = 256
    for start in range(0, pix, step):
        cols = slice(start, start + step)
        p0 = proj_ref[0, :, cols].astype(jnp.float32)
        p1 = proj_ref[1, :, cols].astype(jnp.float32)
        power = (p0 * p0 + p1 * p1).astype(jnp.bfloat16).astype(jnp.float32)
        d0 = jnp.dot(member16, carried_ref[0, :, cols], preferred_element_type=jnp.float32)
        d1 = jnp.dot(member16, carried_ref[1, :, cols], preferred_element_type=jnp.float32)
        dw = jnp.dot(member16, square_ref[:, cols], preferred_element_type=jnp.float32)
        noise_ref[:, cols] = energy_ref[:, cols] + jnp.sum(
            power * dw - 2.0 * (p0 * d0 + p1 * d1), axis=0, keepdims=True
        )
        for i, d in enumerate((d0, d1, dw)):
            table_ref[:, i * classes : (i + 1) * classes, cols] = d.astype(jnp.bfloat16).reshape(
                count // classes, classes, step
            )


def scatter_kernel(shell_vox, vox_dev, index_ref, table_ref, prior_ref, out_ref, total_ref):
    orient = pl.program_id(0)
    groups = vox_dev // LANES
    rows = table_ref.shape[1]

    @pl.when(orient == 0)
    def _():
        total_ref[...] = jnp.zeros_like(total_ref)

    rel = index_ref[pl.ds(orient, 1), :] - voxel_base(shell_vox, vox_dev)
    low = rel & (LANES - 1)
    high = rel >> 8
    pix = rel.shape[1]
    hot = jnp.where(
        lax.broadcasted_iota(jnp.int32, (LANES, pix), 0) == low, 1.0, 0.0
    ).astype(jnp.bfloat16)
    table = table_ref[0]
    parts = [
        table * jnp.where(high == q, 1.0, 0.0).astype(jnp.bfloat16) for q in range(groups)
    ]
    spread = jnp.concatenate(parts, axis=0) if groups > 1 else parts[0]
    total_ref[...] += lax.dot_general(spread, hot, NT, preferred_element_type=jnp.float32)

    @pl.when(orient == pl.num_programs(0) - 1)
    def _():
        third = rows // 3
        for q in range(groups):
            cols = slice(q * LANES, (q + 1) * LANES)
            at = q * rows
            weight = total_ref[at + 2 * third : at + rows, :] + prior_ref[:, cols]
            out_ref[0, :, cols] = (total_ref[at : at + third, :] / weight).astype(jnp.bfloat16)
            out_ref[1, :, cols] = (total_ref[at + third : at + 2 * third, :] / weight).astype(
                jnp.bfloat16
            )


def shards(
    images,
    ctf_gain,
    orientation,
    class_ids,
    slice_index,
    volume,
    noise_power,
    log_prior,
    prior_precision,
):
    groups = lax.axis_size("dom")
    part_dev = images.shape[0]
    pix = images.shape[2]
    classes = volume.shape[0]
    vox_dev = volume.shape[3]
    orients = slice_index.shape[0]
    hypos = classes * orients
    shell_vox = vox_dev * groups
    cands = orientation.shape[1]
    params = pltpu.CompilerParams(vmem_limit_bytes=BIG)
    vol_rows = jnp.transpose(volume[:, :, 0, :], (1, 0, 2)).reshape(2 * classes, vox_dev)
    found = pl.pallas_call(
        functools.partial(gather_kernel, shell_vox, vox_dev),
        grid=(orients,),
        out_shape=jax.ShapeDtypeStruct((2, orients, classes, pix), jnp.bfloat16),
        in_specs=[
            pl.BlockSpec((orients, pix), lambda o: (0, 0)),
            pl.BlockSpec((2 * classes, vox_dev), lambda o: (0, 0)),
        ],
        out_specs=pl.BlockSpec((2, 1, classes, pix), lambda o: (0, o, 0, 0)),
        scratch_shapes=[pltpu.VMEM((2 * classes * vox_dev // LANES, LANES), jnp.bfloat16)],
        compiler_params=params,
    )(slice_index, vol_rows)
    projected = lax.psum(found, "dom").reshape(2, hypos, pix)

    gain = ctf_gain.astype(jnp.float32)
    image0 = images[:, 0, :].astype(jnp.float32)
    image1 = images[:, 1, :].astype(jnp.float32)
    product0 = gain * image0
    product1 = gain * image1
    weighted = jnp.stack([product0 / noise_power, product1 / noise_power]).astype(jnp.bfloat16)
    carried = jnp.stack([product0, product1]).astype(jnp.bfloat16)
    damped = (gain * gain / (2.0 * noise_power)).astype(jnp.bfloat16)
    square = (gain * gain).astype(jnp.bfloat16)
    energy = jnp.sum(image0 * image0 + image1 * image1, axis=0, keepdims=True)
    hypo = (orientation * classes + class_ids).T

    partial_fit = pl.pallas_call(
        fit_kernel,
        out_shape=jax.ShapeDtypeStruct((cands, part_dev), jnp.float32),
        compiler_params=params,
    )(projected, weighted, damped, hypo)
    fitted = lax.psum(partial_fit, "vol")
    vmem = pl.BlockSpec(memory_space=pltpu.VMEM)
    table, noise_part, occ_part = pl.pallas_call(
        member_kernel,
        out_shape=(
            jax.ShapeDtypeStruct((orients, 3 * classes, pix), jnp.bfloat16),
            jax.ShapeDtypeStruct((1, pix), jnp.float32),
            jax.ShapeDtypeStruct((classes, 1), jnp.float32),
        ),
        in_specs=[pl.BlockSpec(memory_space=pltpu.SMEM)] + [vmem] * 6,
        compiler_params=params,
    )(log_prior, fitted, hypo, projected, carried, square, energy)
    table = lax.psum(table, "dom")
    noise_sum, occ_sum = lax.psum((noise_part[0], occ_part[:, 0]), "dom")
    particles = part_dev * groups
    noise_update = noise_sum / (2.0 * particles)
    occupancy = occ_sum / particles
    volume_out = pl.pallas_call(
        functools.partial(scatter_kernel, shell_vox, vox_dev),
        grid=(orients,),
        out_shape=jax.ShapeDtypeStruct((2, classes, vox_dev), jnp.bfloat16),
        in_specs=[
            pl.BlockSpec((orients, pix), lambda o: (0, 0)),
            pl.BlockSpec((1, 3 * classes, pix), lambda o: (o, 0, 0)),
            pl.BlockSpec((1, vox_dev), lambda o: (0, 0)),
        ],
        out_specs=pl.BlockSpec((2, classes, vox_dev), lambda o: (0, 0, 0)),
        scratch_shapes=[pltpu.VMEM((3 * classes * vox_dev // LANES, LANES), jnp.float32)],
        compiler_params=params,
    )(slice_index, table, prior_precision)
    new_volume = jnp.transpose(volume_out, (1, 0, 2))[:, :, None, :]
    return (new_volume, noise_update, occupancy)


def solution(mesh):
    in_specs = (
        P("dom", None, "vol"),
        P("dom", "vol"),
        P("dom", None),
        P("dom", None),
        P(None, "vol"),
        P(None, None, "vol", "dom"),
        P("vol"),
        P(),
        P("vol", "dom"),
    )
    out_specs = (P(None, None, "vol", "dom"), P("vol"), P())
    return jax.shard_map(shards, mesh=mesh, in_specs=in_specs, out_specs=out_specs, check_vma=False)
```

time: 740 us -> 247 us (0.33); the launches traced: 730 us -> 246 us
  local copies, waits for them, and re-layouts: 405 us -> 14.3 us
  other arithmetic: 130 us -> 5.52 us
  Pallas kernels: 0 us -> 23.1 us
  waiting for transfers between devices: 135 us -> 151 us
  matrix products: 7.74 us -> 0 us
    gather x8 -> x0, local copies, waits for them, and re-layouts: 299 us -> none  [the longest x2 265 us: shards(): slices = jnp.take(gathered, local_index, axis=2)]
    psum x0 -> x2, waiting for transfers between devices: none -> 151 us  [the longest x1 88.2 us: shards(): projected = lax.psum(found, 'dom').reshape(2, hypos, pix)]
    scatter-add x1 -> x0, other arithmetic: 101 us -> none  [shards(): jax.ops.segment_sum(values.T, flat_index, num_segments=shell_vox)]
    reduce_scatter x1 -> x0, waiting for transfers between devices: 94.7 us -> none  [shards(): lax.psum_scatter(voxel_rows.T, 'dom', scatter_dimension=1, tiled=True)]
    all_gather x1 -> x0, local copies, waits for them, and re-layouts: 60.3 us -> none  [shards(): gathered = lax.all_gather(volume[:, :, 0, :], 'dom', axis=2, tiled=True)]
    all_gather x1 -> x0, waiting for transfers between devices: 40.6 us -> none  [shards(): gathered = lax.all_gather(volume[:, :, 0, :], 'dom', axis=2, tiled=True)]
    pallas_call x0 -> x4, Pallas kernels: none -> 23.1 us  [the longest x1 10.3 us: shards(): pl.pallas_call(functools.partial(scatter_kernel, shell_vox, vox_dev), gri...]
    scatter-add x1 -> x0, local copies, waits for them, and re-layouts: 23.1 us -> none  [shards(): jax.ops.segment_sum(values.T, flat_index, num_segments=shell_vox)]
where the time goes in v1:
time: 247 us; the launch traced here: 246 us
  waiting for transfers between devices  151 us (61%)
  blocking collectives  38.6 us (16%)
  Pallas kernels  23.1 us (9%)
  local copies, waits for them, and re-layouts  14.3 us (6%)
  between operations  14.2 us (6%)
  other arithmetic  5.52 us (2%)
    psum x1, waiting for transfers between devices, shards(): projected = lax.psum(found, 'dom').reshape(2, hypos, pix)  88.2 us
    psum x1, waiting for transfers between devices, shards(): table = lax.psum(table, 'dom')  62.3 us
    psum x1, blocking collectives, shards(): noise_sum, occ_sum = lax.psum((noise_part[0], occ_part[:, 0]), 'dom')  30.5 us
    pallas_call x1, Pallas kernels, shards(): pl.pallas_call(functools.partial(scatter_kernel, shell_vox, vox_dev), gri...  10.3 us
    unnamed x31, local copies, waits for them, and re-layouts  10.2 us
    pallas_call x1, Pallas kernels, shards(): pl.pallas_call(functools.partial(gather_kernel, shell_vox, vox_dev), grid...  9.05 us
    psum x1, blocking collectives, shards(): fitted = lax.psum(partial_fit, 'vol')  8.13 us
  transfers between devices with their start and end apart: 2, of which 2 were waited for; matrix products, arithmetic and copies ran while one was open for 3% of the time, Pallas kernels for 0%

profile of v1, /device:TPU:0, one launch (start us, length us, event | category | flops | bytes accessed | tf_op | source)
XLA Modules:
  0.0 246.3 jit_solution(1514988773751197137)
XLA Ops:
  7.2 0.0 all-reduce.4.cloned.1.call-start
  7.2 1.1 copy.16
  8.3 0.0 copy-start.6
  8.3 0.8 copy-done.6
  9.2 9.0 %shard_map.112 = bf16[2,16,16,1024]{3,2,1,0:T(8,128)(2,1)} custom-call(s32[16,1024]{1,0:T(8,128)S(1)} %copy-done.6, bf16[32,4096]{1,0:T(8,128)(2,1)S(1)} %bitcast.38), custom_call_target="tpu_custom_call" | custom-call | tf_op jit(solution)/shard_map/pallas_call | solution.py:163
  18.2 0.0 all-reduce.4.cloned.1.call-update
  18.2 0.0 copy-start.12
  18.2 0.0 all-reduce.6.cloned.1.call-start
  18.3 3.0 %fusion.11 = (bf16[512,1,1024]{2,1,0:T(2,128)(2,1)S(1)}, bf16[512,1,1024]{2,1,0:T(2,128)(2,1)S(1)}) fusion(bf16[512,2,1024]{2,1,0:T(2,128)(2,1)S(1)} %copy-done.10), kind=kLoop, calls=%fused_computation.26 | loop fusion | bytes 4194304 | tf_op jit(solution)/shard_map/slice | solution.py:178
  21.3 2.6 %fusion.7 = (bf16[1,512,1024]{2,1,0:T(8,128)(2,1)S(1)}, bf16[1,512,1024]{2,1,0:T(8,128)(2,1)S(1)}, f32[1024]{0:T(1024)S(1)}, bf16[1,512,1024]{2,1,0:T(8,128)(2,1...) fusion(bf16[512,1024]{1,0:T(8,128)(2,1)S(1)} %copy-done.11, ...), kind=kLoop, calls=%fused_computation.16 | loop fusion | flops 9960448 | bytes 9449472 | tf_op jit(solution)/shard_map/stack | solution.py:183
  23.9 1.5 pad_maximum_fusion.weighted_ref
  25.4 0.2 pad_maximum_fusion.1.carried_ref
  25.6 0.5 copy-done.13
  26.1 0.0 copy-done.14
  26.2 88.2 %all-reduce.4.cloned.1.call-done.proj_ref = bf16[2,256,1024]{2,1,0:T(8,128)(2,1)} async-done(((bf16[2,256,1024]{2,1,0:T(8,128)(2,1)}), bf16[2,256,1024]{2,1,0:T(8,128)(2,1)}) %all-reduce.4.cloned.1.call-update) | async-done | bytes 1048592 | tf_op jit(solution)/shard_map/psum | solution.py:175
  114.4 1.6 copy-done
  116.0 1.2 copy-done.1
  117.2 1.2 copy-done.3
  118.4 1.6 shard_map.113
  120.0 8.1 %psum.36.fit_ref = f32[8,512]{1,0:T(8,128)S(1)} all-reduce(f32[8,512]{1,0:T(8,128)S(1)} %shard_map.113), channel_id=1, replica_groups=mesh['dom'=16,'vol'=2] {'vol'}, use_global_device_ids=true, to_apply=%region_1.0 | all-reduce | flops 4096 | bytes 32768 | tf_op jit(solution)/shard_map/psum | solution.py:194
  128.1 1.2 copy-done.2
  129.3 2.2 shard_map.114
  131.5 1.1 copy-done.4
  132.7 0.0 all-reduce.6.cloned.1.call-update
  132.7 0.1 reduce
  132.8 30.5 %all-reduce = (f32[1024]{0:T(1024)S(1)}, f32[16]{0:T(128)S(1)}) all-reduce(f32[1024]{0:T(1024)S(1)} %bitcast.41, f32[16]{0:T(128)S(1)} %reduce), channel_id=1, replica_groups=mesh['dom'=16,'vol'=2] {'dom'}, use_global_device_ids=true, to_apply=%region_4.0 | all-reduce | flops 1040 | bytes 8320 | tf_op jit(solution)/shard_map/psum | solution.py:207
  163.3 0.5 broadcast_multiply_fusion.2
  163.8 0.6 broadcast_multiply_fusion
  164.4 62.3 %all-reduce.6.cloned.1.call-done.table_ref = bf16[16,48,1024]{2,1,0:T(8,128)(2,1)} async-done(((bf16[16,48,1024]{2,1,0:T(8,128)(2,1)}), bf16[16,48,1024]{2,1,0:T(8,128)(2,1)}) %all-reduce.6.cloned.1.call-update) | async-done | bytes 1572880 | tf_op jit(solution)/shard_map/psum | solution.py:206
  226.7 1.4 copy-done.5
  228.2 10.3 %shard_map.115 = bf16[2,16,4096]{2,1,0:T(8,128)(2,1)S(1)} custom-call(s32[16,1024]{1,0:T(8,128)S(1)} %copy-done.7, bf16[16,48,1024]{2,1,0:T(8,128)(2,1)S(1)} %copy-done.5, f32[1,4096]{1,0:T(1,128)S(1)} %copy-done.8), custom_call_target="tpu_custom_call" | custom-call | tf_op jit(solution)/shard_map/pallas_call | solution.py:211
  238.5 1.0 copy.19
  (21 shorter events, 0.0 us)
Async XLA Ops:
  7.2 107.2 %all-reduce.4.cloned.1.call-start = ((), (), s32[]{:S(2)}) async-start(), calls=%async_computation | async-start | bytes 2097152 | tf_op jit(solution)/shard_map/psum | solution.py:175
  8.3 0.8 copy-start.6
  9.2 9.1 %copy-start.10 = (bf16[512,2,1024]{2,1,0:T(2,128)(2,1)S(1)}, bf16[512,2,1024]{2,1,0:T(2,128)(2,1)}, u32[]{:S(2)}) copy-start(bf16[512,2,1024]{2,1,0:T(2,128)(2,1)} %param.9) | copy-start | bytes 6291460
  18.2 3.1 %copy-start.12 = (f32[1024]{0:T(1024)S(1)}, f32[1024]{0:T(1024)}, u32[]{:S(2)}) copy-start(f32[1024]{0:T(1024)} %param.15) | copy-start | bytes 12292
  18.2 208.5 %all-reduce.6.cloned.1.call-start = ((), (), s32[]{:S(2)}) async-start(), calls=%async_computation.1 | async-start | bytes 3145728 | tf_op jit(solution)/shard_map/psum | solution.py:206
  18.3 3.0 %copy-start.11 = (bf16[512,1024]{1,0:T(8,128)(2,1)S(1)}, bf16[512,1024]{1,0:T(8,128)(2,1)}, u32[]{:S(2)}) copy-start(bf16[512,1024]{1,0:T(8,128)(2,1)} %param.10) | copy-start | bytes 3145732
  25.4 0.7 copy-start.13
  25.4 0.7 copy-start.14
  114.4 1.6 copy-start
  116.0 1.2 copy-start.1
  117.2 1.2 copy-start.3
  118.4 9.7 %copy-start.9 = (f32[16]{0:T(128)S(1)}, f32[16]{0:T(128)}, u32[]{:S(2)}) copy-start(f32[16]{0:T(128)} %prior_ref.2) | copy-start | bytes 196
  128.1 1.2 copy-start.2
  129.3 97.4 %copy-start.7 = (s32[16,1024]{1,0:T(8,128)S(1)}, s32[16,1024]{1,0:T(8,128)}, u32[]{:S(2)}) copy-start(s32[16,1024]{1,0:T(8,128)} %index_ref.3) | copy-start | bytes 196612
  129.3 97.4 %copy-start.8 = (f32[1,4096]{1,0:T(1,128)S(1)}, f32[1,4096]{1,0:T(1,128)}, u32[]{:S(2)}) copy-start(f32[1,4096]{1,0:T(1,128)} %prior_ref.3) | copy-start | bytes 49156
  131.5 1.2 copy-start.4
  226.7 1.4 copy-start.5
Sparse Core Ops, SparseCore 0:
  18.4 95.9 all-reduce.3
  132.8 93.8 all-reduce.5

commit v2 on v1

v2 whole, which is shorter than its diff:
```python
import functools

import jax
import jax.numpy as jnp
from jax import lax
from jax.experimental import pallas as pl
from jax.experimental.pallas import tpu as pltpu
from jax.sharding import PartitionSpec as P

LANES = 256
BIG = 48 << 20
NT = (((1,), (1,)), ((), ()))


def voxel_base(shell_vox, vox_dev):
    return lax.axis_index("vol") * shell_vox + lax.axis_index("dom") * vox_dev


def gather_kernel(shell_vox, vox_dev, index_ref, vol_ref, out_ref, stack_ref):
    orient = pl.program_id(0)
    groups = vox_dev // LANES
    rows = vol_ref.shape[0]

    @pl.when(orient == 0)
    def _():
        for q in range(groups):
            stack_ref[q * rows : (q + 1) * rows, :] = vol_ref[:, q * LANES : (q + 1) * LANES]

    rel = index_ref[pl.ds(orient, 1), :] - voxel_base(shell_vox, vox_dev)
    low = rel & (LANES - 1)
    high = rel >> 8
    pix = rel.shape[1]
    step = 256
    for start in range(0, pix, step):
        low_c = low[:, start : start + step]
        high_c = high[:, start : start + step]
        hot = jnp.where(
            lax.broadcasted_iota(jnp.int32, (LANES, step), 0) == low_c, 1.0, 0.0
        ).astype(jnp.bfloat16)
        found = jnp.dot(stack_ref[...], hot, preferred_element_type=jnp.float32)
        total = jnp.zeros((rows, step), jnp.float32)
        for q in range(groups):
            total = jnp.where(high_c == q, found[q * rows : (q + 1) * rows], total)
        out_ref[0, :, start : start + step] = total.astype(jnp.bfloat16)


def scatter_kernel(shell_vox, vox_dev, index_ref, table_ref, prior_ref, out_ref, total_ref):
    orient = pl.program_id(0)
    groups = vox_dev // LANES
    rows = table_ref.shape[1]

    @pl.when(orient == 0)
    def _():
        total_ref[...] = jnp.zeros_like(total_ref)

    rel = index_ref[pl.ds(orient, 1), :] - voxel_base(shell_vox, vox_dev)
    low = rel & (LANES - 1)
    high = rel >> 8
    pix = rel.shape[1]
    hot = jnp.where(
        lax.broadcasted_iota(jnp.int32, (LANES, pix), 0) == low, 1.0, 0.0
    ).astype(jnp.bfloat16)
    table = table_ref[0]
    parts = [
        table * jnp.where(high == q, 1.0, 0.0).astype(jnp.bfloat16) for q in range(groups)
    ]
    spread = jnp.concatenate(parts, axis=0) if groups > 1 else parts[0]
    total_ref[...] += lax.dot_general(spread, hot, NT, preferred_element_type=jnp.float32)

    @pl.when(orient == pl.num_programs(0) - 1)
    def _():
        third = rows // 3
        for q in range(groups):
            cols = slice(q * LANES, (q + 1) * LANES)
            at = q * rows
            weight = total_ref[at + 2 * third : at + rows, :] + prior_ref[:, cols]
            out_ref[0, :, cols] = (total_ref[at : at + third, :] / weight).astype(jnp.bfloat16)
            out_ref[1, :, cols] = (total_ref[at + third : at + 2 * third, :] / weight).astype(
                jnp.bfloat16
            )


MESH = pl.DeviceIdType.MESH
PARTS = 2


def level_bit(level):
    me = lax.axis_index("dom")
    return lax.rem(me // (1 << level), 2)


def partner(level):
    return lax.axis_index("dom") + (1 - 2 * level_bit(level)) * (1 << level)


def greet(levels):
    barrier = pltpu.get_barrier_semaphore()
    for level in range(levels):
        pl.semaphore_signal(barrier, inc=1, device_id={"dom": partner(level)}, device_id_type=MESH)
    pl.semaphore_wait(barrier, levels)


def send(src, dst, send_sem, recv_sem, at, level):
    copy = pltpu.make_async_remote_copy(
        src_ref=src,
        dst_ref=dst,
        send_sem=send_sem.at[at],
        recv_sem=recv_sem.at[at],
        device_id={"dom": partner(level)},
        device_id_type=MESH,
    )
    copy.start()
    return copy


class Exchange:
    def __init__(self, levels, first_ref, full_ref, recv_ref, send_sem, recv_sem):
        self.levels = levels
        self.first, self.full, self.recv = first_ref, full_ref, recv_ref
        self.sems = (send_sem, recv_sem)
        self.width = full_ref.shape[2] // PARTS
        self.low = [0]
        self.size = [1 << levels]
        for level in range(levels):
            half = self.size[-1] // 2
            self.low.append(self.low[-1] + level_bit(level) * half)
            self.size.append(half)
        self.slot = [self.size[0] - self.size[level] for level in range(levels)]

    def cols(self, part):
        return pl.ds(part * self.width, self.width)

    def source(self, level, at):
        if level == 0:
            return self.first, at
        return self.recv, self.slot[level - 1] + at - self.low[level]

    def scatter_start(self, level, part):
        half = self.size[level + 1]
        source, away = self.source(level, self.fresh(level))
        return send(
            source.at[pl.ds(away, half), :, self.cols(part)],
            self.recv.at[pl.ds(self.slot[level], half), :, self.cols(part)],
            *self.sems,
            level * PARTS + part,
            level,
        )

    def scatter_add(self, level, part):
        half = self.size[level + 1]
        for i in range(half):
            source, at = self.source(level, self.low[level + 1] + i)
            slot = self.slot[level] + i
            total = source[at, :, self.cols(part)] + self.recv[slot, :, self.cols(part)]
            if half > 1:
                self.recv[slot, :, self.cols(part)] = total
            else:
                self.full[self.low[level + 1], :, self.cols(part)] = total

    def gather_start(self, level, part):
        held = pl.ds(self.low[level + 1], self.size[level + 1])
        view = self.full.at[held, :, self.cols(part)]
        return send(
            view, view, *self.sems, (self.levels + level) * PARTS + part, level
        )

    def fresh(self, level):
        return self.low[level] + (1 - level_bit(level)) * self.size[level + 1]


def table_kernel(
    shell_vox, vox_dev, levels, index_ref, vol_ref, full_ref,
    stack_ref, first_ref, recv_ref, send_sem, recv_sem,
):
    groups = vox_dev // LANES
    rows = vol_ref.shape[0]
    pix = index_ref.shape[1]
    step = 256
    greet(levels)
    for q in range(groups):
        stack_ref[q * rows : (q + 1) * rows, :] = vol_ref[:, q * LANES : (q + 1) * LANES]
    base = voxel_base(shell_vox, vox_dev)

    def lookup(orient):
        rel = index_ref[pl.ds(orient, 1), :] - base
        low = rel & (LANES - 1)
        high = rel >> 8
        for start in range(0, pix, step):
            low_c = low[:, start : start + step]
            high_c = high[:, start : start + step]
            hot = jnp.where(
                lax.broadcasted_iota(jnp.int32, (LANES, step), 0) == low_c, 1.0, 0.0
            ).astype(jnp.bfloat16)
            found = jnp.dot(stack_ref[...], hot, preferred_element_type=jnp.float32)
            total = jnp.zeros((rows, step), jnp.float32)
            for q in range(groups):
                total = jnp.where(high_c == q, found[q * rows : (q + 1) * rows], total)
            first_ref[orient, :, start : start + step] = total.astype(jnp.bfloat16)

    ex = Exchange(levels, first_ref, full_ref, recv_ref, send_sem, recv_sem)
    half = ex.size[1]
    away = ex.fresh(0)

    @pl.loop(0, half)
    def _(i):
        lookup(away + i)

    copies = [ex.scatter_start(0, part) for part in range(PARTS)]

    @pl.loop(0, half)
    def _(i):
        lookup(ex.low[1] + i)

    for level in range(levels):
        for part in range(PARTS):
            copies[part].wait()
            ex.scatter_add(level, part)
            if level + 1 < levels:
                copies[part] = ex.scatter_start(level + 1, part)
            else:
                copies[part] = ex.gather_start(level, part)
    for level in range(levels - 1, -1, -1):
        for part in range(PARTS):
            copies[part].wait()
            if level > 0:
                copies[part] = ex.gather_start(level - 1, part)


def volume_kernel(
    shell_vox, vox_dev, levels, index_ref, first_ref, small_ref, prior_ref,
    out_ref, small_out_ref,
    total_ref, full_ref, recv_ref, held_ref, got_ref, send_sem, recv_sem, small_send, small_recv,
):
    groups = vox_dev // LANES
    rows = first_ref.shape[1]
    pix = index_ref.shape[1]
    greet(levels)
    base = voxel_base(shell_vox, vox_dev)
    ex = Exchange(levels, first_ref, full_ref, recv_ref, send_sem, recv_sem)
    copies = [ex.scatter_start(0, part) for part in range(PARTS)]
    held_ref[0] = small_ref[...]
    small = send(held_ref.at[0], got_ref.at[0], small_send, small_recv, 0, 0)
    total_ref[...] = jnp.zeros_like(total_ref)

    def spread(orient):
        rel = index_ref[pl.ds(orient, 1), :] - base
        low = rel & (LANES - 1)
        high = rel >> 8
        hot = jnp.where(
            lax.broadcasted_iota(jnp.int32, (LANES, pix), 0) == low, 1.0, 0.0
        ).astype(jnp.bfloat16)
        table = full_ref[orient]
        parts = [
            table * jnp.where(high == q, 1.0, 0.0).astype(jnp.bfloat16) for q in range(groups)
        ]
        wide = jnp.concatenate(parts, axis=0) if groups > 1 else parts[0]
        total_ref[...] += lax.dot_general(wide, hot, NT, preferred_element_type=jnp.float32)

    for level in range(levels):
        for part in range(PARTS):
            copies[part].wait()
            ex.scatter_add(level, part)
            if level + 1 < levels:
                copies[part] = ex.scatter_start(level + 1, part)
            else:
                copies[part] = ex.gather_start(level, part)
        small.wait()
        held_ref[level + 1] = held_ref[level] + got_ref[level]
        if level + 1 < levels:
            small = send(
                held_ref.at[level + 1], got_ref.at[level + 1], small_send, small_recv,
                level + 1, level + 1,
            )
    small_out_ref[...] = held_ref[levels]
    spread(ex.low[levels])
    for level in range(levels - 1, -1, -1):
        for part in range(PARTS):
            copies[part].wait()
            if level > 0:
                copies[part] = ex.gather_start(level - 1, part)

        @pl.loop(0, ex.size[level + 1])
        def _(i, level=level):
            spread(ex.fresh(level) + i)

    third = rows // 3
    for q in range(groups):
        cols = slice(q * LANES, (q + 1) * LANES)
        at = q * rows
        weight = total_ref[at + 2 * third : at + rows, :] + prior_ref[:, cols]
        out_ref[0, :, cols] = (total_ref[at : at + third, :] / weight).astype(jnp.bfloat16)
        out_ref[1, :, cols] = (total_ref[at + third : at + 2 * third, :] / weight).astype(
            jnp.bfloat16
        )


def particle_kernel(
    peers, prior_ref, hypo_ref, table_ref, weighted_ref, damped_ref, carried_ref, square_ref,
    energy_ref, out_ref, small_ref, fits_ref, send_sem, recv_sem,
):
    me = lax.axis_index("vol")
    barrier = pltpu.get_barrier_semaphore()
    for hop in range(1, peers):
        other = lax.rem(me + hop, peers)
        pl.semaphore_signal(barrier, inc=1, device_id={"vol": other}, device_id_type=MESH)
    orients, double, pix = table_ref.shape
    classes = double // 2
    count = orients * classes
    step = 256
    hypo = hypo_ref[...]
    value = jnp.zeros((count, hypo.shape[1]), jnp.float32)

    def views(cols):
        p0 = table_ref[:, :classes, cols].reshape(count, step)
        p1 = table_ref[:, classes:, cols].reshape(count, step)
        f0 = p0.astype(jnp.float32)
        f1 = p1.astype(jnp.float32)
        return p0, p1, f0, f1, (f0 * f0 + f1 * f1).astype(jnp.bfloat16)

    for start in range(0, pix, step):
        cols = slice(start, start + step)
        p0, p1, _, _, power = views(cols)
        value += lax.dot_general(p0, weighted_ref[0, :, cols], NT, preferred_element_type=jnp.float32)
        value += lax.dot_general(p1, weighted_ref[1, :, cols], NT, preferred_element_type=jnp.float32)
        value -= lax.dot_general(power, damped_ref[:, cols], NT, preferred_element_type=jnp.float32)
    ids = lax.broadcasted_iota(jnp.int32, value.shape, 0)
    rows = [
        jnp.sum(jnp.where(hypo[k : k + 1, :] == ids, value, 0.0), axis=0, keepdims=True)
        for k in range(hypo.shape[0])
    ]
    fits_ref[me] = jnp.concatenate(rows, axis=0)
    pl.semaphore_wait(barrier, peers - 1)
    copies = []
    for hop in range(1, peers):
        copy = pltpu.make_async_remote_copy(
            src_ref=fits_ref.at[me],
            dst_ref=fits_ref.at[me],
            send_sem=send_sem.at[hop - 1],
            recv_sem=recv_sem.at[hop - 1],
            device_id={"vol": lax.rem(me + hop, peers)},
            device_id_type=MESH,
        )
        copy.start()
        copies.append(copy)
    class_of = lax.rem(hypo, classes)
    scores = jnp.zeros(hypo.shape, jnp.float32)
    for c in range(classes):
        scores += jnp.where(class_of == c, prior_ref[c], 0.0)
    for copy in copies:
        copy.wait()
    fit = fits_ref[0]
    for peer in range(1, peers):
        fit += fits_ref[peer]
    scores += fit
    top = jnp.max(scores, axis=0, keepdims=True)
    expo = jnp.exp(scores - top)
    posterior = expo / jnp.sum(expo, axis=0, keepdims=True)
    member = jnp.zeros(ids.shape, jnp.float32)
    for k in range(hypo.shape[0]):
        member += jnp.where(hypo[k : k + 1, :] == ids, posterior[k : k + 1, :], 0.0)
    occ = jnp.sum(member, axis=1, keepdims=True)
    occ = jnp.sum(occ.reshape(orients, classes, 1), axis=0)
    noise_rows = pix // 128
    small_ref[noise_rows:, :] = jnp.broadcast_to(occ, (classes, 128))
    member16 = member.astype(jnp.bfloat16)
    for start in range(0, pix, step):
        cols = slice(start, start + step)
        _, _, f0, f1, power = views(cols)
        d0 = jnp.dot(member16, carried_ref[0, :, cols], preferred_element_type=jnp.float32)
        d1 = jnp.dot(member16, carried_ref[1, :, cols], preferred_element_type=jnp.float32)
        dw = jnp.dot(member16, square_ref[:, cols], preferred_element_type=jnp.float32)
        noise = energy_ref[:, cols] + jnp.sum(
            power.astype(jnp.float32) * dw - 2.0 * (f0 * d0 + f1 * d1), axis=0, keepdims=True
        )
        for i in range(step // 128):
            row = start // 128 + i
            small_ref[row : row + 1, :] = noise[:, i * 128 : (i + 1) * 128]
        for i, d in enumerate((d0, d1, dw)):
            out_ref[:, i * classes : (i + 1) * classes, cols] = d.astype(jnp.bfloat16).reshape(
                orients, classes, step
            )


def shards(
    images,
    ctf_gain,
    orientation,
    class_ids,
    slice_index,
    volume,
    noise_power,
    log_prior,
    prior_precision,
):
    groups = lax.axis_size("dom")
    peers = lax.axis_size("vol")
    part_dev = images.shape[0]
    pix = images.shape[2]
    classes = volume.shape[0]
    vox_dev = volume.shape[3]
    orients = slice_index.shape[0]
    shell_vox = vox_dev * groups
    cands = orientation.shape[1]
    levels = groups.bit_length() - 1
    direct = groups == orients and groups == 1 << levels
    params = pltpu.CompilerParams(vmem_limit_bytes=BIG)
    vmem = pl.BlockSpec(memory_space=pltpu.VMEM)
    vol_rows = jnp.transpose(volume[:, :, 0, :], (1, 0, 2)).reshape(2 * classes, vox_dev)
    stack = pltpu.VMEM((2 * classes * vox_dev // LANES, LANES), jnp.bfloat16)
    if direct:
        table = pl.pallas_call(
            functools.partial(table_kernel, shell_vox, vox_dev, levels),
            out_shape=jax.ShapeDtypeStruct((orients, 2 * classes, pix), jnp.bfloat16),
            in_specs=[vmem] * 2,
            out_specs=vmem,
            scratch_shapes=[
                stack,
                pltpu.VMEM((orients, 2 * classes, pix), jnp.bfloat16),
                pltpu.VMEM((orients - 1, 2 * classes, pix), jnp.bfloat16),
                pltpu.SemaphoreType.DMA((2 * levels * PARTS,)),
                pltpu.SemaphoreType.DMA((2 * levels * PARTS,)),
            ],
            compiler_params=pltpu.CompilerParams(
                vmem_limit_bytes=BIG, collective_id=0, has_side_effects=True
            ),
        )(slice_index, vol_rows)
    else:
        found = pl.pallas_call(
            functools.partial(gather_kernel, shell_vox, vox_dev),
            grid=(orients,),
            out_shape=jax.ShapeDtypeStruct((orients, 2 * classes, pix), jnp.bfloat16),
            in_specs=[
                pl.BlockSpec((orients, pix), lambda o: (0, 0)),
                pl.BlockSpec((2 * classes, vox_dev), lambda o: (0, 0)),
            ],
            out_specs=pl.BlockSpec((1, 2 * classes, pix), lambda o: (o, 0, 0)),
            scratch_shapes=[stack],
            compiler_params=params,
        )(slice_index, vol_rows)
        table = lax.psum(found, "dom")

    gain = ctf_gain.astype(jnp.float32)
    image0 = images[:, 0, :].astype(jnp.float32)
    image1 = images[:, 1, :].astype(jnp.float32)
    product0 = gain * image0
    product1 = gain * image1
    weighted = jnp.stack([product0 / noise_power, product1 / noise_power]).astype(jnp.bfloat16)
    carried = jnp.stack([product0, product1]).astype(jnp.bfloat16)
    damped = (gain * gain / (2.0 * noise_power)).astype(jnp.bfloat16)
    square = (gain * gain).astype(jnp.bfloat16)
    energy = jnp.sum(image0 * image0 + image1 * image1, axis=0, keepdims=True)
    hypo = (orientation * classes + class_ids).T

    noise_rows = pix // 128
    sums, small = pl.pallas_call(
        functools.partial(particle_kernel, peers),
        out_shape=(
            jax.ShapeDtypeStruct((orients, 3 * classes, pix), jnp.bfloat16),
            jax.ShapeDtypeStruct((noise_rows + classes, 128), jnp.float32),
        ),
        in_specs=[pl.BlockSpec(memory_space=pltpu.SMEM)] + [vmem] * 7,
        out_specs=(vmem, vmem),
        scratch_shapes=[
            pltpu.VMEM((peers, cands, part_dev), jnp.float32),
            pltpu.SemaphoreType.DMA((peers - 1,)),
            pltpu.SemaphoreType.DMA((peers - 1,)),
        ],
        compiler_params=pltpu.CompilerParams(
            vmem_limit_bytes=BIG, collective_id=1, has_side_effects=True
        ),
    )(log_prior, hypo, table, weighted, damped, carried, square, energy)
    out_shape = jax.ShapeDtypeStruct((2, classes, vox_dev), jnp.bfloat16)
    total = pltpu.VMEM((3 * classes * vox_dev // LANES, LANES), jnp.float32)
    if direct:
        volume_out, small = pl.pallas_call(
            functools.partial(volume_kernel, shell_vox, vox_dev, levels),
            out_shape=(out_shape, jax.ShapeDtypeStruct(small.shape, jnp.float32)),
            in_specs=[vmem] * 4,
            out_specs=(vmem, vmem),
            scratch_shapes=[
                total,
                pltpu.VMEM((orients, 3 * classes, pix), jnp.bfloat16),
                pltpu.VMEM((orients - 1, 3 * classes, pix), jnp.bfloat16),
                pltpu.VMEM((levels + 1,) + small.shape, jnp.float32),
                pltpu.VMEM((levels,) + small.shape, jnp.float32),
                pltpu.SemaphoreType.DMA((2 * levels * PARTS,)),
                pltpu.SemaphoreType.DMA((2 * levels * PARTS,)),
                pltpu.SemaphoreType.DMA((levels,)),
                pltpu.SemaphoreType.DMA((levels,)),
            ],
            compiler_params=pltpu.CompilerParams(
                vmem_limit_bytes=BIG, collective_id=2, has_side_effects=True
            ),
        )(slice_index, sums, small, prior_precision)
    else:
        small = lax.psum(small, "dom")
        volume_out = pl.pallas_call(
            functools.partial(scatter_kernel, shell_vox, vox_dev),
            grid=(orients,),
            out_shape=out_shape,
            in_specs=[
                pl.BlockSpec((orients, pix), lambda o: (0, 0)),
                pl.BlockSpec((1, 3 * classes, pix), lambda o: (o, 0, 0)),
                pl.BlockSpec((1, vox_dev), lambda o: (0, 0)),
            ],
            out_specs=pl.BlockSpec((2, classes, vox_dev), lambda o: (0, 0, 0)),
            scratch_shapes=[total],
            compiler_params=params,
        )(slice_index, lax.psum(sums, "dom"), prior_precision)
    particles = part_dev * groups
    noise_update = small[:noise_rows].reshape(pix) / (2.0 * particles)
    occupancy = small[noise_rows:, 0] / particles
    new_volume = jnp.transpose(volume_out, (1, 0, 2))[:, :, None, :]
    return (new_volume, noise_update, occupancy)


def solution(mesh):
    in_specs = (
        P("dom", None, "vol"),
        P("dom", "vol"),
        P("dom", None),
        P("dom", None),
        P(None, "vol"),
        P(None, None, "vol", "dom"),
        P("vol"),
        P(),
        P("vol", "dom"),
    )
    out_specs = (P(None, None, "vol", "dom"), P("vol"), P())
    return jax.shard_map(shards, mesh=mesh, in_specs=in_specs, out_specs=out_specs, check_vma=False)
```

time: 247 us -> 106 us (0.43)
  waiting for transfers between devices: 151 us -> 0 us
  Pallas kernels: 23.1 us -> 93.2 us
  blocking collectives: 38.6 us -> 0 us
  between operations: 14.2 us -> 0.81 us
  local copies, waits for them, and re-layouts: 14.3 us -> 7.06 us
    psum x2 -> x0, waiting for transfers between devices: 151 us -> none  [the longest x1 88.2 us: shards(): projected = lax.psum(found, 'dom').reshape(2, hypos, pix)]
    pallas_call x4 -> x3, Pallas kernels: 23.1 us -> 93.2 us  [the longest x1 45.6 us: shards(): pl.pallas_call(functools.partial(volume_kernel, shell_vox, vox_dev, level...]
    psum x2 -> x0, blocking collectives: 38.6 us -> none  [the longest x1 30.5 us: shards(): noise_sum, occ_sum = lax.psum((noise_part[0], occ_part[:, 0]), 'dom')]
    unnamed x31 -> x17, local copies, waits for them, and re-layouts: 10.2 us -> 1.02 us
    slice x1, local copies, waits for them, and re-layouts: 2.98 us -> 5.89 us  [shards(): image0 = images[:, 0, :].astype(jnp.float32)]
  transfers between devices with their start and end apart: 2 -> 0, of which waited for: 2 -> 0; matrix products, arithmetic and copies ran while one was open for 3% -> 0% of each run, Pallas kernels for 0% -> 0%
where the time goes in v2:
time: 106 us
  Pallas kernels  93.2 us (88%)
  local copies, waits for them, and re-layouts  7.06 us (7%)
  other arithmetic  5.17 us (5%)
    pallas_call x1, Pallas kernels, shards(): pl.pallas_call(functools.partial(volume_kernel, shell_vox, vox_dev, level...  45.6 us
    pallas_call x1, Pallas kernels, shards(): pl.pallas_call(functools.partial(table_kernel, shell_vox, vox_dev, levels...  38.6 us
    pallas_call x1, Pallas kernels, shards(): pl.pallas_call(functools.partial(particle_kernel, peers), out_shape=(jax....  8.92 us
    slice x1, local copies, waits for them, and re-layouts, shards(): image0 = images[:, 0, :].astype(jnp.float32)  5.89 us
    another operation x1, other arithmetic, shards(): jnp.stack([product0 / noise_power, product1 / noise_power])  2.31 us

profile of v2, /device:TPU:0, one launch (start us, length us, event | category | flops | bytes accessed | tf_op | source)
XLA Modules:
  0.0 106.2 jit_solution(4478679708797703025)
XLA Ops:
  0.6 0.0 copy-start.5
  0.6 0.0 copy-start.3
  0.7 5.9 %fusion.11 = (bf16[512,1,1024]{2,1,0:T(2,128)(2,1)S(1)}, bf16[512,1,1024]{2,1,0:T(2,128)(2,1)S(1)}) fusion(bf16[512,2,1024]{2,1,0:T(2,128)(2,1)} %param.9), kind=kLoop, calls=%fused_computation.26 | loop fusion | bytes 4194304 | tf_op jit(solution)/shard_map/slice | solution.py:443
  6.5 0.0 copy-done.5
  6.6 0.0 copy-done.3
  6.6 1.6 %fusion.7 = (bf16[1,512,1024]{2,1,0:T(8,128)(2,1)S(1)}, bf16[1,512,1024]{2,1,0:T(8,128)(2,1)S(1)}, f32[1024]{0:T(1024)S(1)}, bf16[1,512,1024]{2,1,0:T(8,128)(2,1...) fusion(bf16[512,1024]{1,0:T(8,128)(2,1)S(1)} %copy-done.3, ...), kind=kLoop, calls=%fused_computation.16 | loop fusion | flops 9960448 | bytes 9449472 | tf_op jit(solution)/shard_map/stack | solution.py:448
  8.2 0.0 copy-start.4
  8.2 0.0 copy-start
  8.2 0.0 copy-start.6
  8.2 0.0 copy-start.7
  8.3 0.0 copy-start.2
  8.3 2.3 %pad_maximum_fusion = (bf16[2,512,1024]{2,1,0:T(8,128)(2,1)}, bf16[2,512,1024]{2,1,0:T(8,128)(2,1)}) fusion(bf16[1,512,1024]{2,1,0:T(8,128)(2,1)S(1)} %get-tuple-element.20, bf16[1,512,1024]{2,1,0:T(8,128)(2,1)S(1)} %get-tuple-element.22, bf16[1,512,1024]{2,1,0:T(8,128)(2,1)S(1)} %get-tuple-element.19, bf16[1,512,1024]{2,1,0:T(8,128)(2,1)S(1)} %get-tuple-element.23), kind=kLoop, calls=%fused_computation.10 | loop fusion | flops 2097152 | bytes 8388608 | tf_op jit(solution)/shard_map/stack | solution.py:447
  10.6 0.0 copy-done.4
  10.6 0.1 copy.16
  10.7 0.0 copy-done
  10.7 38.6 %shard_map.112.table_ref = bf16[16,32,1024]{2,1,0:T(8,128)(2,1)S(1)} custom-call(s32[16,1024]{1,0:T(8,128)S(1)} %copy-done, bf16[32,4096]{1,0:T(8,128)(2,1)S(1)} %bitcast.38), custom_call_target="tpu_custom_call" | custom-call | tf_op jit(solution)/shard_map/pallas_call | solution.py:411
  49.4 0.0 copy-done.6
  49.4 0.0 copy-done.7
  49.4 0.0 copy-done.2
  49.4 0.0 copy-start.1
  49.5 8.9 %shard_map.113 = (bf16[16,48,1024]{2,1,0:T(8,128)(2,1)S(1)}, f32[24,128]{1,0:T(8,128)S(1)}) custom-call(f32[16]{0:T(128)S(1)} %copy-done.2, s32[8,512]{1,0:T(8,128)S(1)} %add_bitcast_fusion.hypo_ref, bf16[16,32,1024]{2,1,0:T(8,128)(2,1)S(1)} %shard_map.112.table_ref, bf16[2,512,1024]{2,1,0:T(8,128)(2,1)} %get-tuple-element.28.weighted_ref, ...), custom_call_target="tpu_custom_call" | custom-call | tf_op jit(solution)/shard_map/pallas_call | solution.py:455
  58.4 0.0 copy-done.1
  58.4 45.6 %shard_map.114 = (bf16[2,16,4096]{2,1,0:T(8,128)(2,1)S(1)}, f32[24,128]{1,0:T(8,128)S(1)}) custom-call(s32[16,1024]{1,0:T(8,128)S(1)} %copy-done, bf16[16,48,1024]{2,1,0:T(8,128)(2,1)S(1)} %get-tuple-element.7.first_ref, f32[24,128]{1,0:T(8,128)S(1)} %get-tuple-element.8.small_ref, f32[1,4096]{1,0:T(1,128)S(1)} %copy-done.1), custom_call_target="tpu_custom_call" | custom-call | tf_op jit(solution)/shard_map/pallas_call | solution.py:475
  104.0 1.0 copy.19
  105.0 0.6 multiply_bitcast_fusion
  105.6 0.6 multiply_reduce_fusion
  (2 shorter events, 0.0 us)
Async XLA Ops:
  0.6 5.9 %copy-start.5 = (f32[1024]{0:T(1024)S(1)}, f32[1024]{0:T(1024)}, u32[]{:S(2)}) copy-start(f32[1024]{0:T(1024)} %param.15) | copy-start | bytes 12292
  0.6 5.9 %copy-start.3 = (bf16[512,1024]{1,0:T(8,128)(2,1)S(1)}, bf16[512,1024]{1,0:T(8,128)(2,1)}, u32[]{:S(2)}) copy-start(bf16[512,1024]{1,0:T(8,128)(2,1)} %param.10) | copy-start | bytes 3145732
  8.2 2.4 %copy-start.4 = (bf16[16,2,1,4096]{3,1,2,0:T(2,128)(2,1)S(1)}, bf16[16,2,1,4096]{3,1,2,0:T(2,128)(2,1)}, u32[]{:S(2)}) copy-start(bf16[16,2,1,4096]{3,1,2,0:T(2,128)(2,1)} %param.14) | copy-start | bytes 786436
  8.2 2.5 %copy-start = (s32[16,1024]{1,0:T(8,128)S(1)}, s32[16,1024]{1,0:T(8,128)}, u32[]{:S(2)}) copy-start(s32[16,1024]{1,0:T(8,128)} %index_ref.3) | copy-start | bytes 196612
  8.2 41.2 %copy-start.6 = (s32[512,8]{0,1:T(8,128)S(1)}, s32[512,8]{0,1:T(8,128)}, u32[]{:S(2)}) copy-start(s32[512,8]{0,1:T(8,128)} %param.12) | copy-start | bytes 49156
  8.2 41.2 %copy-start.7 = (s32[512,8]{0,1:T(8,128)S(1)}, s32[512,8]{0,1:T(8,128)}, u32[]{:S(2)}) copy-start(s32[512,8]{0,1:T(8,128)} %param.11) | copy-start | bytes 49156
  8.3 41.2 %copy-start.2 = (f32[16]{0:T(128)S(1)}, f32[16]{0:T(128)}, u32[]{:S(2)}) copy-start(f32[16]{0:T(128)} %prior_ref.2) | copy-start | bytes 196
  49.4 8.9 %copy-start.1 = (f32[1,4096]{1,0:T(1,128)S(1)}, f32[1,4096]{1,0:T(1,128)}, u32[]{:S(2)}) copy-start(f32[1,4096]{1,0:T(1,128)} %prior_ref.3) | copy-start | bytes 49156

commit v3 on v2

--- a/solution.py
+++ b/solution.py
@@ -168,15 +168,14 @@
         return self.low[level] + (1 - level_bit(level)) * self.size[level + 1]
 
 
-def table_kernel(
+def exchange_table(
     shell_vox, vox_dev, levels, index_ref, vol_ref, full_ref,
-    stack_ref, first_ref, recv_ref, send_sem, recv_sem,
+    stack_ref, first_ref, recv_ref, send_sem, recv_sem, prepare, chunks,
 ):
     groups = vox_dev // LANES
     rows = vol_ref.shape[0]
     pix = index_ref.shape[1]
     step = 256
-    greet(levels)
     for q in range(groups):
         stack_ref[q * rows : (q + 1) * rows, :] = vol_ref[:, q * LANES : (q + 1) * LANES]
     base = voxel_base(shell_vox, vox_dev)
@@ -212,6 +211,8 @@
         lookup(ex.low[1] + i)
 
     for level in range(levels):
+        if level == 1:
+            pl.loop(0, chunks // 2)(prepare)
         for part in range(PARTS):
             copies[part].wait()
             ex.scatter_add(level, part)
@@ -220,6 +221,8 @@
             else:
                 copies[part] = ex.gather_start(level, part)
     for level in range(levels - 1, -1, -1):
+        if level == min(1, levels - 1):
+            pl.loop(chunks // 2, chunks)(prepare)
         for part in range(PARTS):
             copies[part].wait()
             if level > 0:
@@ -295,14 +298,49 @@
 
 
 def particle_kernel(
-    peers, prior_ref, hypo_ref, table_ref, weighted_ref, damped_ref, carried_ref, square_ref,
-    energy_ref, out_ref, small_ref, fits_ref, send_sem, recv_sem,
+    peers, dims, prior_ref, hypo_ref, image0_ref, image1_ref, gain_ref, noise_ref, index_ref,
+    source_ref, out_ref, small_ref, fits_ref, weighted_ref, damped_ref, carried_ref, square_ref,
+    energy_ref, send_sem, recv_sem, *scratch,
 ):
     me = lax.axis_index("vol")
     barrier = pltpu.get_barrier_semaphore()
+    greeted = peers - 1
+    if dims is not None:
+        greeted += dims[2]
+        for level in range(dims[2]):
+            pl.semaphore_signal(
+                barrier, inc=1, device_id={"dom": partner(level)}, device_id_type=MESH
+            )
     for hop in range(1, peers):
         other = lax.rem(me + hop, peers)
         pl.semaphore_signal(barrier, inc=1, device_id={"vol": other}, device_id_type=MESH)
+    pl.semaphore_wait(barrier, greeted)
+    inverse = 1.0 / noise_ref[...]
+    energy_ref[...] = jnp.zeros_like(energy_ref)
+    block = 32
+    chunks = gain_ref.shape[0] // block
+
+    def prepare(i):
+        rows = pl.ds(pl.multiple_of(i * block, block), block)
+        gain = gain_ref[rows, :].astype(jnp.float32)
+        square = gain * gain
+        square_ref[rows, :] = square.astype(jnp.bfloat16)
+        damped_ref[rows, :] = (square * (0.5 * inverse)).astype(jnp.bfloat16)
+        power = jnp.zeros(gain.shape, jnp.float32)
+        for r, image_ref in enumerate((image0_ref, image1_ref)):
+            image = image_ref[rows, :].astype(jnp.float32)
+            power += image * image
+            product = gain * image
+            carried_ref[r, rows, :] = product.astype(jnp.bfloat16)
+            weighted_ref[r, rows, :] = (product * inverse).astype(jnp.bfloat16)
+        energy_ref[...] += jnp.sum(power.reshape(block // 8, 8, -1), axis=0)
+
+    if dims is None:
+        table_ref = source_ref
+        pl.loop(0, chunks)(prepare)
+    else:
+        table_ref = scratch[0]
+        exchange_table(*dims, index_ref, source_ref, *scratch, prepare, chunks)
     orients, double, pix = table_ref.shape
     classes = double // 2
     count = orients * classes
@@ -329,7 +367,6 @@
         for k in range(hypo.shape[0])
     ]
     fits_ref[me] = jnp.concatenate(rows, axis=0)
-    pl.semaphore_wait(barrier, peers - 1)
     copies = []
     for hop in range(1, peers):
         copy = pltpu.make_async_remote_copy(
@@ -369,7 +406,7 @@
         d0 = jnp.dot(member16, carried_ref[0, :, cols], preferred_element_type=jnp.float32)
         d1 = jnp.dot(member16, carried_ref[1, :, cols], preferred_element_type=jnp.float32)
         dw = jnp.dot(member16, square_ref[:, cols], preferred_element_type=jnp.float32)
-        noise = energy_ref[:, cols] + jnp.sum(
+        noise = jnp.sum(energy_ref[:, cols], axis=0, keepdims=True) + jnp.sum(
             power.astype(jnp.float32) * dw - 2.0 * (f0 * d0 + f1 * d1), axis=0, keepdims=True
         )
         for i in range(step // 128):
@@ -407,23 +444,28 @@
     vmem = pl.BlockSpec(memory_space=pltpu.VMEM)
     vol_rows = jnp.transpose(volume[:, :, 0, :], (1, 0, 2)).reshape(2 * classes, vox_dev)
     stack = pltpu.VMEM((2 * classes * vox_dev // LANES, LANES), jnp.bfloat16)
+    particle_scratch = [
+        pltpu.VMEM((peers, cands, part_dev), jnp.float32),
+        pltpu.VMEM((2, part_dev, pix), jnp.bfloat16),
+        pltpu.VMEM((part_dev, pix), jnp.bfloat16),
+        pltpu.VMEM((2, part_dev, pix), jnp.bfloat16),
+        pltpu.VMEM((part_dev, pix), jnp.bfloat16),
+        pltpu.VMEM((8, pix), jnp.float32),
+        pltpu.SemaphoreType.DMA((peers - 1,)),
+        pltpu.SemaphoreType.DMA((peers - 1,)),
+    ]
+    dims = None
+    source = vol_rows
     if direct:
-        table = pl.pallas_call(
-            functools.partial(table_kernel, shell_vox, vox_dev, levels),
-            out_shape=jax.ShapeDtypeStruct((orients, 2 * classes, pix), jnp.bfloat16),
-            in_specs=[vmem] * 2,
-            out_specs=vmem,
-            scratch_shapes=[
-                stack,
-                pltpu.VMEM((orients, 2 * classes, pix), jnp.bfloat16),
-                pltpu.VMEM((orients - 1, 2 * classes, pix), jnp.bfloat16),
-                pltpu.SemaphoreType.DMA((2 * levels * PARTS,)),
-                pltpu.SemaphoreType.DMA((2 * levels * PARTS,)),
-            ],
-            compiler_params=pltpu.CompilerParams(
-                vmem_limit_bytes=BIG, collective_id=0, has_side_effects=True
-            ),
-        )(slice_index, vol_rows)
+        dims = (shell_vox, vox_dev, levels)
+        particle_scratch += [
+            pltpu.VMEM((orients, 2 * classes, pix), jnp.bfloat16),
+            stack,
+            pltpu.VMEM((orients, 2 * classes, pix), jnp.bfloat16),
+            pltpu.VMEM((orients - 1, 2 * classes, pix), jnp.bfloat16),
+            pltpu.SemaphoreType.DMA((2 * levels * PARTS,)),
+            pltpu.SemaphoreType.DMA((2 * levels * PARTS,)),
+        ]
     else:
         found = pl.pallas_call(
             functools.partial(gather_kernel, shell_vox, vox_dev),
@@ -437,38 +479,26 @@
             scratch_shapes=[stack],
             compiler_params=params,
         )(slice_index, vol_rows)
-        table = lax.psum(found, "dom")
-
-    gain = ctf_gain.astype(jnp.float32)
-    image0 = images[:, 0, :].astype(jnp.float32)
-    image1 = images[:, 1, :].astype(jnp.float32)
-    product0 = gain * image0
-    product1 = gain * image1
-    weighted = jnp.stack([product0 / noise_power, product1 / noise_power]).astype(jnp.bfloat16)
-    carried = jnp.stack([product0, product1]).astype(jnp.bfloat16)
-    damped = (gain * gain / (2.0 * noise_power)).astype(jnp.bfloat16)
-    square = (gain * gain).astype(jnp.bfloat16)
-    energy = jnp.sum(image0 * image0 + image1 * image1, axis=0, keepdims=True)
+        source = lax.psum(found, "dom")
+
     hypo = (orientation * classes + class_ids).T
-
     noise_rows = pix // 128
     sums, small = pl.pallas_call(
-        functools.partial(particle_kernel, peers),
+        functools.partial(particle_kernel, peers, dims),
         out_shape=(
             jax.ShapeDtypeStruct((orients, 3 * classes, pix), jnp.bfloat16),
             jax.ShapeDtypeStruct((noise_rows + classes, 128), jnp.float32),
         ),
         in_specs=[pl.BlockSpec(memory_space=pltpu.SMEM)] + [vmem] * 7,
         out_specs=(vmem, vmem),
-        scratch_shapes=[
-            pltpu.VMEM((peers, cands, part_dev), jnp.float32),
-            pltpu.SemaphoreType.DMA((peers - 1,)),
-            pltpu.SemaphoreType.DMA((peers - 1,)),
-        ],
+        scratch_shapes=particle_scratch,
         compiler_params=pltpu.CompilerParams(
             vmem_limit_bytes=BIG, collective_id=1, has_side_effects=True
         ),
-    )(log_prior, hypo, table, weighted, damped, carried, square, energy)
+    )(
+        log_prior, hypo, images[:, 0, :], images[:, 1, :], ctf_gain, noise_power[None, :],
+        slice_index, source,
+    )
     out_shape = jax.ShapeDtypeStruct((2, classes, vox_dev), jnp.bfloat16)
     total = pltpu.VMEM((3 * classes * vox_dev // LANES, LANES), jnp.float32)
     if direct:

time: 106 us -> 101 us (0.953)
  other arithmetic: 5.17 us -> 1.23 us
  Pallas kernels: 93.2 us -> 91.3 us
    another operation x2 -> x0, other arithmetic: 3.94 us -> none  [the longest x1 2.31 us: shards(): jnp.stack([product0 / noise_power, product1 / noise_power])]
    pallas_call x2 -> x1, Pallas kernels: 47.6 us -> 45.7 us  [shards(): pl.pallas_call(functools.partial(particle_kernel, peers, dims), out_shape...]
where the time goes in v3:
time: 101 us
  Pallas kernels  91.3 us (90%)
  local copies, waits for them, and re-layouts  8.02 us (8%)
  other arithmetic  1.23 us (1%)
    pallas_call x1, Pallas kernels, shards(): pl.pallas_call(functools.partial(particle_kernel, peers, dims), out_shape...  45.7 us
    pallas_call x1, Pallas kernels, shards(): pl.pallas_call(functools.partial(volume_kernel, shell_vox, vox_dev, level...  45.6 us
    slice x1, local copies, waits for them, and re-layouts, shards(): images[:, 1, :]  5.78 us

profile of v3, /device:TPU:0, one launch (start us, length us, event | category | flops | bytes accessed | tf_op | source)
XLA Modules:
  0.0 101.3 jit_solution(885962889603182668)
XLA Ops:
  0.6 5.8 %fusion = (bf16[512,1,1024]{2,1,0:T(2,128)(2,1)S(1)}, bf16[512,1,1024]{2,1,0:T(2,128)(2,1)S(1)}) fusion(bf16[512,2,1024]{2,1,0:T(2,128)(2,1)} %param.9), kind=kLoop, calls=%fused_computation.5 | loop fusion | bytes 4194304 | tf_op jit(solution)/shard_map/slice | solution.py:499
  6.4 0.0 copy-start.5
  6.4 0.0 copy-start.6
  6.4 0.0 copy-start.7
  6.5 0.0 copy-start
  6.5 0.0 copy-start.1
  6.5 0.0 copy-start.3
  6.5 0.0 copy-start.4
  6.5 0.8 copy_bitcast_fusion
  7.3 0.0 copy-start.2
  7.3 0.0 copy-done.5
  7.4 0.1 copy.18
  7.5 0.0 copy-done.6
  7.5 0.0 copy-done.7
  7.6 0.2 copy-done
  7.8 0.0 copy-done.1
  7.8 0.0 copy-done.3
  7.8 0.0 copy-done.4
  7.8 45.7 %shard_map.112 = (bf16[16,48,1024]{2,1,0:T(8,128)(2,1)S(1)}, f32[24,128]{1,0:T(8,128)S(1)}) custom-call(f32[16]{0:T(128)S(1)} %copy-done.4, s32[8,512]{1,0:T(8,128)S(1)} %add_bitcast_fusion.hypo_ref, bf16[512,1024]{1,0:T(8,128)(2,1)S(1)} %get-tuple-element.20.image0_ref, bf16[512,1024]{1,0:T(8,128)(2,1)S(1)} %get-tuple-element.19.image1_ref, ...), custom_call_target="tpu_custom_call" | custom-call | tf_op jit(solution)/shard_map/pallas_call | solution.py:486
  53.5 0.0 copy-done.2
  53.5 45.6 %shard_map.113 = (bf16[2,16,4096]{2,1,0:T(8,128)(2,1)S(1)}, f32[24,128]{1,0:T(8,128)S(1)}) custom-call(s32[16,1024]{1,0:T(8,128)S(1)} %copy-done.1, bf16[16,48,1024]{2,1,0:T(8,128)(2,1)S(1)} %get-tuple-element.7.first_ref, f32[24,128]{1,0:T(8,128)S(1)} %get-tuple-element.8.small_ref, f32[1,4096]{1,0:T(1,128)S(1)} %copy-done.2), custom_call_target="tpu_custom_call" | custom-call | tf_op jit(solution)/shard_map/pallas_call | solution.py:505
  99.1 0.6 multiply_bitcast_fusion
  99.7 0.6 multiply_reduce_fusion
  100.3 1.0 copy.19
  (1 shorter events, 0.0 us)
Async XLA Ops:
  6.4 1.0 copy-start.5
  6.4 1.1 %copy-start.6 = (s32[512,8]{0,1:T(8,128)S(1)}, s32[512,8]{0,1:T(8,128)}, u32[]{:S(2)}) copy-start(s32[512,8]{0,1:T(8,128)} %param.12) | copy-start | bytes 49156
  6.4 1.1 %copy-start.7 = (s32[512,8]{0,1:T(8,128)S(1)}, s32[512,8]{0,1:T(8,128)}, u32[]{:S(2)}) copy-start(s32[512,8]{0,1:T(8,128)} %param.11) | copy-start | bytes 49156
  6.5 1.3 %copy-start = (bf16[512,1024]{1,0:T(8,128)(2,1)S(1)}, bf16[512,1024]{1,0:T(8,128)(2,1)}, u32[]{:S(2)}) copy-start(bf16[512,1024]{1,0:T(8,128)(2,1)} %gain_ref.1) | copy-start | bytes 3145732
  6.5 1.3 %copy-start.1 = (s32[16,1024]{1,0:T(8,128)S(1)}, s32[16,1024]{1,0:T(8,128)}, u32[]{:S(2)}) copy-start(s32[16,1024]{1,0:T(8,128)} %index_ref.3) | copy-start | bytes 196612
  6.5 1.3 %copy-start.3 = (f32[1024]{0:T(1024)S(1)}, f32[1024]{0:T(1024)}, u32[]{:S(2)}) copy-start(f32[1024]{0:T(1024)} %param.15) | copy-start | bytes 12292
  6.5 1.3 %copy-start.4 = (f32[16]{0:T(128)S(1)}, f32[16]{0:T(128)}, u32[]{:S(2)}) copy-start(f32[16]{0:T(128)} %prior_ref.2) | copy-start | bytes 196
  7.3 46.1 %copy-start.2 = (f32[1,4096]{1,0:T(1,128)S(1)}, f32[1,4096]{1,0:T(1,128)}, u32[]{:S(2)}) copy-start(f32[1,4096]{1,0:T(1,128)} %prior_ref.3) | copy-start | bytes 49156
